TPU v7x, 256 devices: a whole 4x4x8 slice. The times are simulated.
256 devices in a mesh: dp: 32 (over x, z), ctx: 8 (over y, core).
Axes of the slice: x: 4, y: 4, z: 8, core: 2. Of those that a mesh axis runs over, the one named last changes fastest.
Arguments:
- layer_input: bfloat16 [32, 1024, 4096], P('dp', 'ctx'), may hold values from -6 to 6
- queries: bfloat16 [32, 1024, 4096], P('dp', 'ctx'), may hold values from -4.5 to 4.5
- keys_saved: bfloat16 [32, 1024, 1024], P('dp', 'ctx'), may hold values from -4.5 to 4.5
- values_saved: bfloat16 [32, 1024, 1024], P('dp', 'ctx'), may hold values from -6 to 6
- out_grad: bfloat16 [32, 1024, 4096], P('dp', 'ctx'), may hold values from -6 to 6
- master_weight: float32 [4096, 6144], P('dp', 'ctx'), may hold values from -2 to 2
- first_moment: float32 [4096, 6144], P('dp', 'ctx'), may hold values from -100 to 100
- second_moment: float32 [4096, 6144], P('dp', 'ctx'), may hold values from 10 to 3000
Outputs:
- first_new: float32 [4096, 6144], P('dp', 'ctx')
- second_new: float32 [4096, 6144], P('dp', 'ctx')
- lamb_update: float32 [4096, 6144], P('dp', 'ctx')
- new_weights: bfloat16 [4096, 6144], P(None, 'ctx')
All inputs are finite; a program needn't handle non-finite values.
Results may differ from a plain program's by a relative error of at most 0.0095.
Values may be sent and summed in bfloat16 or wider, within the bound.
No kernel may reach another device: no remote copies, remote signals or barrier semaphores. Data moves between devices by JAX's collectives and lax.ppermute only.
A program may use at most 128 MiB of HBM per device.

v0:
```python
import jax
import jax.numpy as jnp
from jax import lax
from jax.sharding import PartitionSpec as P

HEAD_DIM = 128
STEP = 100
beta_first = 0.9
beta_second = 0.999
adam_epsilon = 1e-06
decay_rate = 0.01
learn_rate = 0.01
masked_score = -1e30


def head_grads(query_local, key_local, value_local, grad_local):
    length = query_local.shape[0]
    kv_local = key_local.shape[1] // HEAD_DIM
    group_size = query_local.shape[1] // key_local.shape[1]
    block_rows = min(512, length)
    block_count = length // block_rows
    score_scale = HEAD_DIM ** (-0.5)
    query_blocks = query_local.reshape(block_count, block_rows, kv_local, group_size, HEAD_DIM)
    grad_blocks = grad_local.reshape(block_count, block_rows, kv_local, group_size, HEAD_DIM)
    key_rows = key_local.reshape(length, kv_local, HEAD_DIM)
    value_rows = value_local.reshape(length, kv_local, HEAD_DIM)
    positions = jnp.arange(length)

    def one_block(accums, block_items):
        key_acc, value_acc = accums
        query_blk, grad_blk, block_start = block_items
        scores = (
            jnp.einsum("qgrd,kgd->grqk", query_blk, key_rows, preferred_element_type=jnp.float32)
            * score_scale
        )
        query_pos = block_start + jnp.arange(block_rows)
        allowed = positions[None, :] <= query_pos[:, None]
        scores = jnp.where(allowed, scores, masked_score)
        row_max = jnp.max(scores, axis=-1, keepdims=True)
        weights = jnp.exp(scores - row_max)
        probabilities = weights / jnp.sum(weights, axis=-1, keepdims=True)
        probs_b = probabilities.astype(jnp.bfloat16)
        attended = jnp.einsum(
            "grqk,kgd->qgrd", probs_b, value_rows, preferred_element_type=jnp.float32
        )
        row_delta = jnp.sum(grad_blk.astype(jnp.float32) * attended, axis=-1)
        prob_grad = jnp.einsum(
            "qgrd,kgd->grqk", grad_blk, value_rows, preferred_element_type=jnp.float32
        )
        dscore = (
            probabilities * (prob_grad - jnp.transpose(row_delta, (1, 2, 0))[..., None])
        ).astype(jnp.bfloat16)
        query_grad = (
            jnp.einsum("grqk,kgd->qgrd", dscore, key_rows, preferred_element_type=jnp.float32)
            * score_scale
        ).astype(jnp.bfloat16)
        key_acc = key_acc + jnp.einsum(
            "grqk,qgrd->kgd", dscore, query_blk, preferred_element_type=jnp.float32
        )
        value_acc = value_acc + jnp.einsum(
            "grqk,qgrd->kgd", probs_b, grad_blk, preferred_element_type=jnp.float32
        )
        return ((key_acc, value_acc), query_grad)

    starts = jnp.arange(block_count) * block_rows
    empty_acc = jnp.zeros((length, kv_local, HEAD_DIM), jnp.float32)
    (key_acc, value_acc), query_grads = lax.scan(
        one_block, (empty_acc, empty_acc), (query_blocks, grad_blocks, starts)
    )
    query_grad = query_grads.reshape(length, kv_local, group_size * HEAD_DIM)
    key_grad = (key_acc * score_scale).astype(jnp.bfloat16)
    value_grad = value_acc.astype(jnp.bfloat16)
    return jnp.concatenate([query_grad, key_grad, value_grad], axis=2).reshape(length, -1)


def body(
    layer_input,
    queries,
    keys_saved,
    values_saved,
    out_grad,
    master_weight,
    first_moment,
    second_moment,
):
    weight_sq = jnp.sum(master_weight * master_weight)
    query_heads, key_heads, value_heads, grad_heads = (
        lax.all_to_all(queries, "ctx", split_axis=2, concat_axis=1, tiled=True),
        lax.all_to_all(keys_saved, "ctx", split_axis=2, concat_axis=1, tiled=True),
        lax.all_to_all(values_saved, "ctx", split_axis=2, concat_axis=1, tiled=True),
        lax.all_to_all(out_grad, "ctx", split_axis=2, concat_axis=1, tiled=True),
    )
    grouped = head_grads(query_heads[0], key_heads[0], value_heads[0], grad_heads[0])
    partial_value = lax.dot_general(
        lax.all_gather(layer_input, "ctx", axis=1, tiled=True)[0],
        grouped,
        (((0,), (0,)), ((), ())),
        preferred_element_type=jnp.float32,
    )
    gradient = lax.psum_scatter(
        partial_value.astype(jnp.bfloat16), "dp", scatter_dimension=0, tiled=True
    ).astype(jnp.float32)
    first_new = beta_first * first_moment + (1.0 - beta_first) * gradient
    second_new = beta_second * second_moment + (1.0 - beta_second) * gradient * gradient
    corr_first = 1.0 - beta_first**STEP
    corr_second = 1.0 - beta_second**STEP
    direction = (
        first_new / corr_first / (jnp.sqrt(second_new / corr_second) + adam_epsilon)
        + decay_rate * master_weight
    )
    update_sq = jnp.sum(direction * direction)
    weight_total, update_total = lax.psum((weight_sq, update_sq), ("dp", "ctx"))
    trust_ratio = jnp.sqrt(weight_total) / jnp.sqrt(update_total)
    lamb_update = trust_ratio * direction
    new_local = (master_weight - learn_rate * lamb_update).astype(jnp.bfloat16)
    new_weights = lax.all_gather(new_local, "dp", axis=0, tiled=True)
    return (first_new, second_new, lamb_update, new_weights)


def solution(mesh):
    in_specs = (
        P("dp", "ctx", None),
        P("dp", "ctx", None),
        P("dp", "ctx", None),
        P("dp", "ctx", None),
        P("dp", "ctx", None),
        P("dp", "ctx"),
        P("dp", "ctx"),
        P("dp", "ctx"),
    )
    out_specs = (P("dp", "ctx"), P("dp", "ctx"), P("dp", "ctx"), P(None, "ctx"))
    return jax.shard_map(body, mesh=mesh, in_specs=in_specs, out_specs=out_specs, check_vma=False)
```

profile of v0, /device:TPU:36, one launch (start us, length us, event | category | flops | bytes accessed | tf_op | source)
XLA Modules:
  0.0 623.9 jit_solution(10160004014047542531)
XLA Ops:
  11.9 4.5 all-to-all-start.3
  23.9 4.0 all-to-all-start.1
  28.0 5.0 copy.102
  33.0 22.4 %reduce.3 = bf16[4096,128]{1,0:T(8,128)(2,1)S(1)} reduce(bf16[4096,1,128]{2,1,0:T(2,128)(2,1)S(1)} %bitcast.220, bf16[]{:T(256)} %broadcast.70), dimensions={1}, to_apply=%bitcast.150.reduce_sub_computation | reduce | bytes 2097154
  56.6 4.7 all-to-all-start
  61.2 5.0 copy.106
  66.3 23.4 %reduce.5 = bf16[4096,128]{1,0:T(8,128)(2,1)} reduce(bf16[4096,1,128]{2,1,0:T(2,128)(2,1)S(1)} %bitcast.219, bf16[]{:T(256)} %broadcast.70), dimensions={1}, to_apply=%bitcast.154.reduce_sub_computation | reduce | bytes 2097154
  91.9 4.8 all-to-all-start.2
  100.3 4.3 reshape.108
  107.5 5.3 all-to-all-done.2
  112.7 5.9 reshape.112
  123.8 66.4 %while.15 = (s32[]{:T(128)}, f32[1024,1,128]{0,2,1:T(8,128)S(1)}, f32[1024,1,128]{0,2,1:T(8,128)}, bf16[2,512,1,4,128]{4,3,1,0,2:T(4,128)(2,1)}, bf16[2,512,1,4,...) while((s32[]{:T(128)}, f32[1024,1,128]{0,2,1:T(8,128)S(1)}, ...), condition=%wide.region_4.5_spmd.clone, body=%wide.region_0.4_spmd.clone.sunk | while | flops 3273910784 | bytes 178353008 | solution.py:67
  134.9 5.3 fusion.84
  141.1 3.5 fusion.85
  149.1 7.3 %fusion.87 = f32[1024,1,128]{0,2,1:T(8,128)} fusion(bf16[1,512,1,4,128]{4,3,1,0,2:T(4,128)(2,1)S(1)} %get-tuple-element.238, f32[1024,1,128]{0,2,1:T(8,128)} %get-tuple-element.255, pred[]{:T(512)S(6)} %compare.3, f32[4,512]{1,0:T(4,128)S(1)} %fusion.83, f32[4,512]{1,0:T(4,128)S(1)} %get-tuple-element.241, f32[512,4,1024]{2,0,1:T(8,128)} %copy-done, ...), kind=kOutput, calls=%fused_computation.23.clone.1 | convolution fusion | flops 547618816 | bytes 10502145 | tf_op jit(solution)/shard_map/while/body/eval_jaxpr/grqk,qgrd->kgd/dot_general | solution.py:60
  168.3 5.3 fusion.84
  174.2 3.5 fusion.85
  182.2 7.2 %fusion.87 = f32[1024,1,128]{0,2,1:T(8,128)} fusion(bf16[1,512,1,4,128]{4,3,1,0,2:T(4,128)(2,1)S(1)} %get-tuple-element.238, f32[1024,1,128]{0,2,1:T(8,128)} %get-tuple-element.255, pred[]{:T(512)S(6)} %compare.3, f32[4,512]{1,0:T(4,128)S(1)} %fusion.83, f32[4,512]{1,0:T(4,128)S(1)} %get-tuple-element.241, f32[512,4,1024]{2,0,1:T(8,128)} %copy-done, ...), kind=kOutput, calls=%fused_computation.23.clone.1 | convolution fusion | flops 547618816 | bytes 10502145 | tf_op jit(solution)/shard_map/while/body/eval_jaxpr/grqk,qgrd->kgd/dot_general | solution.py:60
  193.5 12.3 %fusion.45 = bf16[4096,768]{0,1:T(8,128)(2,1)} fusion(bf16[1,1024,4096]{2,1,0:T(8,128)(2,1)} %all-gather.3.cloned.1.call-done, bf16[1024,1,128]{2,0,1:T(8,128)(2,1)S(1)} %copy.115, bf16[1024,1,128]{2,0,1:T(8,128)(2,1)S(1)} %multiply_convert_fusion, bf16[1024,1,512]{2,0,1:T(8,128)(2,1)S(1)} %reshape.90), kind=kOutput, calls=%fused_computation.42 | convolution fusion | flops 6450315264 | bytes 16252928 | tf_op jit(solution)/shard_map/dot_general | solution.py:94
  205.8 8.7 %copy.129 = bf16[4096,768]{1,0:T(8,128)(2,1)} copy(bf16[4096,768]{0,1:T(8,128)(2,1)} %fusion.45) | data formatting | bytes 12582912
  215.8 222.4 %reduce-scatter.4.cloned.1.call-done = bf16[128,768]{1,0:T(8,128)(2,1)} async-done(((bf16[4096,768]{1,0:T(8,128)(2,1)}), bf16[128,768]{1,0:T(8,128)(2,1)}) %reduce-scatter.4.cloned.1.call-update) | async-done | bytes 196624
  440.2 74.4 %all-reduce = (f32[]{:T(128)}, f32[]{:T(128)}) all-reduce(f32[]{:T(128)} %multiply_reduce_fusion.1, f32[]{:T(128)} %get-tuple-element.171), channel_id=1, replica_groups=mesh['dp'=32,'ctx'=8] {'dp','ctx'}, use_global_device_ids=true, to_apply=%region_7.8 | all-reduce | flops 2 | bytes 16 | tf_op jit(solution)/shard_map/psum | solution.py:112
  519.6 89.2 %all-gather.5.cloned.1.call-done = bf16[4096,768]{0,1:T(8,128)(2,1)} async-done(((bf16[128,768]{0,1:T(8,128)(2,1)}), bf16[4096,768]{0,1:T(8,128)(2,1)}) %all-gather.5.cloned.1.call-update) | async-done | bytes 6291472 | tf_op jit(solution)/shard_map/all_gather | solution.py:116
  608.8 8.6 %copy.122 = bf16[4096,768]{1,0:T(8,128)(2,1)} copy(bf16[4096,768]{0,1:T(8,128)(2,1)} %all-gather.5.cloned.1.call-done) | data formatting | bytes 12582912
  (106 shorter events, 71.2 us)
Async XLA Ops:
  11.9 12.0 %all-to-all-start.3 = ((bf16[8,2,8192]{2,1,0:T(2,128)(2,1)}), bf16[8,2,8192]{2,1,0:T(2,128)(2,1)S(1)}, u32[]{:S(2)}, u32[]{:S(2)}) async-start(bf16[8,2,8192]{2,1,0:T(2,128)(2,1)} %reshape.113), calls=%async_computation.3 | async-start | bytes 524288 | tf_op jit(solution)/shard_map/all_to_all | solution.py:90
  23.9 32.6 %all-to-all-start.1 = ((bf16[8,2,8192]{2,1,0:T(2,128)(2,1)}), bf16[8,2,8192]{2,1,0:T(2,128)(2,1)}, u32[]{:S(2)}, u32[]{:S(2)}) async-start(bf16[8,2,8192]{2,1,0:T(2,128)(2,1)} %reshape.109), calls=%async_computation.1 | async-start | bytes 524288 | tf_op jit(solution)/shard_map/all_to_all | solution.py:89
  56.6 35.3 %all-to-all-start = ((bf16[8,2,32768]{2,1,0:T(2,128)(2,1)}), bf16[8,2,32768]{2,1,0:T(2,128)(2,1)S(1)}, u32[]{:S(2)}, u32[]{:S(2)}) async-start(bf16[8,2,32768]{2,1,0:T(2,128)(2,1)} %reshape.107), calls=%async_computation | async-start | bytes 2097152 | tf_op jit(solution)/shard_map/all_to_all | solution.py:88
  91.9 8.2 %copy-start.6 = (bf16[8,2,32768]{2,1,0:T(2,128)(2,1)}, bf16[8,2,32768]{2,1,0:T(2,128)(2,1)S(1)}, u32[]{:S(2)}) copy-start(bf16[8,2,32768]{2,1,0:T(2,128)(2,1)S(1)} %all-to-all-done) | copy-start | bytes 3145732
  91.9 20.9 %all-to-all-start.2 = ((bf16[8,2,32768]{2,1,0:T(2,128)(2,1)}), bf16[8,2,32768]{2,1,0:T(2,128)(2,1)}, u32[]{:S(2)}, u32[]{:S(2)}) async-start(bf16[8,2,32768]{2,1,0:T(2,128)(2,1)} %reshape.111), calls=%async_computation.2 | async-start | bytes 2097152 | tf_op jit(solution)/shard_map/all_to_all | solution.py:91
  96.7 96.8 %all-gather.3.cloned.1.call-start = ((), (), s32[]{:S(2)}) async-start(), calls=%async_computation.5 | async-start | bytes 9437184 | tf_op jit(solution)/shard_map/all_gather | solution.py:95
  97.4 340.8 %reduce-scatter.4.cloned.1.call-start = ((), (), s32[]{:S(2)}) async-start(), calls=%async_computation.7 | async-start | bytes 6488064
  123.8 10.7 %copy-start.4 = (bf16[2,512,1,4,128]{4,3,1,0,2:T(4,128)(2,1)}, bf16[2,512,1,4,128]{4,3,1,0,2:T(4,128)(2,1)S(1)}, u32[]{:S(2)}) copy-start(bf16[2,512,1,4,128]{4,3,1,0,2:T(4,128)(2,1)S(1)} %get-tuple-element.268) | copy-start | bytes 3145732 | tf_op jit(solution)/shard_map/while
  128.8 3.2 copy-start
  134.8 6.2 %copy-start.1 = (f32[512,4,1024]{2,0,1:T(8,128)S(1)}, f32[512,4,1024]{2,0,1:T(8,128)}, u32[]{:S(2)}) copy-start(f32[512,4,1024]{2,0,1:T(8,128)} %copy-done) | copy-start | bytes 25165828 | tf_op jit(solution)/shard_map/while
  134.8 6.2 copy-start.10
  144.6 2.0 copy-start.2
  149.1 7.3 %copy-start.3 = (bf16[4,512,1024]{2,1,0:T(8,128)(2,1)S(1)}, bf16[4,512,1024]{2,1,0:T(8,128)(2,1)}, u32[]{:S(2)}) copy-start(bf16[4,512,1024]{2,1,0:T(8,128)(2,1)} %copy-done.2) | copy-start | bytes 12582916 | tf_op jit(solution)/shard_map/while
  149.1 8.1 %copy-start.5 = (bf16[2,512,1,4,128]{4,3,1,0,2:T(4,128)(2,1)S(1)}, bf16[2,512,1,4,128]{4,3,1,0,2:T(4,128)(2,1)}, u32[]{:S(2)}) copy-start(bf16[2,512,1,4,128]{4,3,1,0,2:T(4,128)(2,1)} %copy-done.4) | copy-start | bytes 3145732 | tf_op jit(solution)/shard_map/while
  157.2 10.7 %copy-start.4 = (bf16[2,512,1,4,128]{4,3,1,0,2:T(4,128)(2,1)}, bf16[2,512,1,4,128]{4,3,1,0,2:T(4,128)(2,1)S(1)}, u32[]{:S(2)}) copy-start(bf16[2,512,1,4,128]{4,3,1,0,2:T(4,128)(2,1)S(1)} %get-tuple-element.268) | copy-start | bytes 3145732 | tf_op jit(solution)/shard_map/while
  162.2 3.2 copy-start
  168.2 5.9 copy-start.1
  168.2 5.9 copy-start.10
  182.2 7.3 %copy-start.3 = (bf16[4,512,1024]{2,1,0:T(8,128)(2,1)S(1)}, bf16[4,512,1024]{2,1,0:T(8,128)(2,1)}, u32[]{:S(2)}) copy-start(bf16[4,512,1024]{2,1,0:T(8,128)(2,1)} %copy-done.2) | copy-start | bytes 12582916 | tf_op jit(solution)/shard_map/while
  182.2 8.1 %copy-start.5 = (bf16[2,512,1,4,128]{4,3,1,0,2:T(4,128)(2,1)S(1)}, bf16[2,512,1,4,128]{4,3,1,0,2:T(4,128)(2,1)}, u32[]{:S(2)}) copy-start(bf16[2,512,1,4,128]{4,3,1,0,2:T(4,128)(2,1)} %copy-done.4) | copy-start | bytes 3145732 | tf_op jit(solution)/shard_map/while
  205.7 8.8 %copy-start.7 = (f32[128,768]{1,0:T(8,128)S(1)}, f32[128,768]{1,0:T(8,128)}, u32[]{:S(2)}) copy-start(f32[128,768]{1,0:T(8,128)} %param.15) | copy-start | bytes 1179652
  205.7 9.0 %copy-start.8 = (f32[128,768]{1,0:T(8,128)S(1)}, f32[128,768]{1,0:T(8,128)}, u32[]{:S(2)}) copy-start(f32[128,768]{1,0:T(8,128)} %param.16) | copy-start | bytes 1179652
  205.7 9.2 %copy-start.9 = (f32[128,768]{1,0:T(8,128)S(1)}, f32[128,768]{1,0:T(8,128)}, u32[]{:S(2)}) copy-start(f32[128,768]{1,0:T(8,128)} %param.17) | copy-start | bytes 1179652
  214.5 394.2 %all-gather.5.cloned.1.call-start = ((), (), s32[]{:S(2)}) async-start(), calls=%async_computation.6 | async-start | bytes 6488064 | tf_op jit(solution)/shard_map/all_gather | solution.py:116
  (1 other events, 2.0 us)
Sparse Core Ops, SparseCore 0:
  99.4 55.1 all-gather.2
  214.6 223.5 reduce-scatter.3
  516.9 91.7 all-gather.4
where the time goes:
time: 626 us; the launch traced here: 624 us
  waiting for transfers between devices  321 us (51%)
  local copies, waits for them, and re-layouts  83 us (13%)
  blocking collectives  74.4 us (12%)
  other arithmetic  59.6 us (10%)
  matrix products  52.3 us (8%)
  starting transfers between devices  18.1 us (3%)
  between operations  15.4 us (2%)
    unnamed x4, waiting for transfers between devices  223 us
    all_gather x1, waiting for transfers between devices, body(): new_weights = lax.all_gather(new_local, 'dp', axis=0, tiled=True)  89.2 us
    psum x1, blocking collectives, body(): weight_total, update_total = lax.psum((weight_sq, update_sq), ('dp', 'ctx'))  74.4 us
    unnamed x35, local copies, waits for them, and re-layouts  55 us
    unnamed x6, other arithmetic  50.2 us
    dot_general x2, matrix products, one_block(): jnp.einsum('grqk,qgrd->kgd', probs_b, grad_blk, preferred_element_type=jn...  14.5 us
  transfers between devices with their start and end apart: 7, of which 4 were waited for; matrix products, arithmetic and copies ran while one was open for 23% of the time, Pallas kernels for 0%

commit v1 on v0

--- a/solution.py
+++ b/solution.py
@@ -113,7 +113,9 @@
     trust_ratio = jnp.sqrt(weight_total) / jnp.sqrt(update_total)
     lamb_update = trust_ratio * direction
     new_local = (master_weight - learn_rate * lamb_update).astype(jnp.bfloat16)
-    new_weights = lax.all_gather(new_local, "dp", axis=0, tiled=True)
+    new_weights = jnp.concatenate(
+        lax.all_to_all(jnp.stack([new_local] * lax.axis_size("dp")), "dp", 0, 0), axis=0
+    )
     return (first_new, second_new, lamb_update, new_weights)
 
 

time: 626 us -> 684 us (1.093)
  waiting for transfers between devices: 321 us -> 368 us
  starting transfers between devices: 18.1 us -> 26.8 us
    all_to_all x0 -> x1, waiting for transfers between devices: none -> 136 us  [body(): lax.all_to_all(jnp.stack([new_local] * lax.axis_size('dp')), 'dp', 0, 0)]
    all_gather x1 -> x0, waiting for transfers between devices: 89.2 us -> none  [body(): new_weights = lax.all_gather(new_local, 'dp', axis=0, tiled=True)]
    all_to_all x0 -> x1, starting transfers between devices: none -> 8.69 us  [body(): lax.all_to_all(jnp.stack([new_local] * lax.axis_size('dp')), 'dp', 0, 0)]
    unnamed x4 -> x3, waiting for transfers between devices: 223 us -> 224 us
  transfers between devices with their start and end apart: 7 -> 7, of which waited for: 4 -> 4; matrix products, arithmetic and copies ran while one was open for 23% -> 21% of each run, Pallas kernels for 0% -> 0%
where the time goes in v1:
time: 684 us; the launch traced here: 680 us
  waiting for transfers between devices  368 us (54%)
  local copies, waits for them, and re-layouts  83.9 us (12%)
  blocking collectives  74.2 us (11%)
  other arithmetic  58.9 us (9%)
  matrix products  52.3 us (8%)
  starting transfers between devices  26.8 us (4%)
  between operations  15.7 us (2%)
    unnamed x3, waiting for transfers between devices  224 us
    all_to_all x1, waiting for transfers between devices, body(): lax.all_to_all(jnp.stack([new_local] * lax.axis_size('dp')), 'dp', 0, 0)  136 us
    psum x1, blocking collectives, body(): weight_total, update_total = lax.psum((weight_sq, update_sq), ('dp', 'ctx'))  74.2 us
    unnamed x35, local copies, waits for them, and re-layouts  52.3 us
    unnamed x6, other arithmetic  50.2 us
    dot_general x2, matrix products, one_block(): jnp.einsum('grqk,qgrd->kgd', probs_b, grad_blk, preferred_element_type=jn...  14.5 us
  transfers between devices with their start and end apart: 7, of which 4 were waited for; matrix products, arithmetic and copies ran while one was open for 21% of the time, Pallas kernels for 0%

profile of v1, /device:TPU:36, one launch (start us, length us, event | category | flops | bytes accessed | tf_op | source)
XLA Modules:
  0.0 680.1 jit_solution(7198667600995544776)
XLA Ops:
  11.9 4.5 all-to-all-start.3
  23.9 4.1 all-to-all-start.1
  28.0 5.0 copy.102
  33.0 22.4 %reduce.3 = bf16[4096,128]{1,0:T(8,128)(2,1)S(1)} reduce(bf16[4096,1,128]{2,1,0:T(2,128)(2,1)S(1)} %bitcast.221, bf16[]{:T(256)} %broadcast.72), dimensions={1}, to_apply=%bitcast.151.reduce_sub_computation | reduce | bytes 2097154
  56.6 4.7 all-to-all-start
  61.2 5.0 copy.106
  66.3 23.4 %reduce.5 = bf16[4096,128]{1,0:T(8,128)(2,1)} reduce(bf16[4096,1,128]{2,1,0:T(2,128)(2,1)S(1)} %bitcast.220, bf16[]{:T(256)} %broadcast.72), dimensions={1}, to_apply=%bitcast.155.reduce_sub_computation | reduce | bytes 2097154
  91.9 4.8 all-to-all-start.2
  100.3 4.3 reshape.114
  107.5 5.3 all-to-all-done.2
  112.8 5.9 reshape.118
  123.9 66.5 %while.15 = (s32[]{:T(128)}, f32[1024,1,128]{0,2,1:T(8,128)S(1)}, f32[1024,1,128]{0,2,1:T(8,128)}, bf16[2,512,1,4,128]{4,3,1,0,2:T(4,128)(2,1)}, bf16[2,512,1,4,...) while((s32[]{:T(128)}, f32[1024,1,128]{0,2,1:T(8,128)S(1)}, ...), condition=%wide.region_4.5_spmd.clone, body=%wide.region_0.4_spmd.clone.sunk | while | flops 3273910784 | bytes 178353008 | solution.py:67
  134.9 5.3 fusion.84
  141.1 3.5 fusion.85
  149.2 7.3 %fusion.87 = f32[1024,1,128]{0,2,1:T(8,128)} fusion(bf16[1,512,1,4,128]{4,3,1,0,2:T(4,128)(2,1)S(1)} %get-tuple-element.238, f32[1024,1,128]{0,2,1:T(8,128)} %get-tuple-element.255, pred[]{:T(512)S(6)} %compare.3, f32[4,512]{1,0:T(4,128)S(1)} %fusion.83, f32[4,512]{1,0:T(4,128)S(1)} %get-tuple-element.241, f32[512,4,1024]{2,0,1:T(8,128)} %copy-done, ...), kind=kOutput, calls=%fused_computation.23.clone.1 | convolution fusion | flops 547618816 | bytes 10502145 | tf_op jit(solution)/shard_map/while/body/eval_jaxpr/grqk,qgrd->kgd/dot_general | solution.py:60
  168.3 5.3 fusion.84
  182.3 7.3 %fusion.87 = f32[1024,1,128]{0,2,1:T(8,128)} fusion(bf16[1,512,1,4,128]{4,3,1,0,2:T(4,128)(2,1)S(1)} %get-tuple-element.238, f32[1024,1,128]{0,2,1:T(8,128)} %get-tuple-element.255, pred[]{:T(512)S(6)} %compare.3, f32[4,512]{1,0:T(4,128)S(1)} %fusion.83, f32[4,512]{1,0:T(4,128)S(1)} %get-tuple-element.241, f32[512,4,1024]{2,0,1:T(8,128)} %copy-done, ...), kind=kOutput, calls=%fused_computation.23.clone.1 | convolution fusion | flops 547618816 | bytes 10502145 | tf_op jit(solution)/shard_map/while/body/eval_jaxpr/grqk,qgrd->kgd/dot_general | solution.py:60
  193.5 12.3 %fusion.45 = bf16[4096,768]{0,1:T(8,128)(2,1)} fusion(bf16[1,1024,4096]{2,1,0:T(8,128)(2,1)} %all-gather.2.cloned.1.call-done, bf16[1024,1,128]{2,0,1:T(8,128)(2,1)S(1)} %copy.115, bf16[1024,1,128]{2,0,1:T(8,128)(2,1)S(1)} %multiply_convert_fusion, bf16[1024,1,512]{2,0,1:T(8,128)(2,1)S(1)} %reshape.95), kind=kOutput, calls=%fused_computation.42 | convolution fusion | flops 6450315264 | bytes 16252928 | tf_op jit(solution)/shard_map/dot_general | solution.py:94
  205.8 8.8 %copy.129 = bf16[4096,768]{1,0:T(8,128)(2,1)} copy(bf16[4096,768]{0,1:T(8,128)(2,1)} %fusion.45) | data formatting | bytes 12582912
  215.8 222.9 %reduce-scatter.4.cloned.1.call-done = bf16[128,768]{1,0:T(8,128)(2,1)} async-done(((bf16[4096,768]{1,0:T(8,128)(2,1)}), bf16[128,768]{1,0:T(8,128)(2,1)}) %reduce-scatter.4.cloned.1.call-update) | async-done | bytes 196624
  440.8 74.2 %all-reduce = (f32[]{:T(128)}, f32[]{:T(128)}) all-reduce(f32[]{:T(128)} %multiply_reduce_fusion.1, f32[]{:T(128)} %get-tuple-element.171), channel_id=1, replica_groups=mesh['dp'=32,'ctx'=8] {'dp','ctx'}, use_global_device_ids=true, to_apply=%region_7.8 | all-reduce | flops 2 | bytes 16 | tf_op jit(solution)/shard_map/psum | solution.py:112
  520.0 8.7 %all-to-all-start.4 = ((bf16[32,128,768]{2,1,0:T(8,128)(2,1)}), bf16[32,128,768]{2,1,0:T(8,128)(2,1)}, u32[]{:S(2)}, u32[]{:S(2)}) async-start(bf16[32,128,768]{2,1,0:T(8,128)(2,1)} %stack.2), calls=%async_computation.4 | async-start | bytes 12582912 | tf_op jit(solution)/shard_map/all_to_all | solution.py:117
  531.4 135.9 %all-to-all-done.4 = bf16[32,128,768]{2,1,0:T(8,128)(2,1)} async-done(((bf16[32,128,768]{2,1,0:T(8,128)(2,1)}), bf16[32,128,768]{2,1,0:T(8,128)(2,1)}, u32[]{:S(2)}, u32[]{:S(2)}) %all-to-all-start.4) | async-done | bytes 6291488 | tf_op jit(solution)/shard_map/all_to_all | solution.py:117
  667.4 5.9 copy.179
  (107 shorter events, 77.5 us)
Async XLA Ops:
  11.9 12.0 %all-to-all-start.3 = ((bf16[8,2,8192]{2,1,0:T(2,128)(2,1)}), bf16[8,2,8192]{2,1,0:T(2,128)(2,1)S(1)}, u32[]{:S(2)}, u32[]{:S(2)}) async-start(bf16[8,2,8192]{2,1,0:T(2,128)(2,1)} %reshape.119), calls=%async_computation.3 | async-start | bytes 524288 | tf_op jit(solution)/shard_map/all_to_all | solution.py:90
  23.9 32.6 %all-to-all-start.1 = ((bf16[8,2,8192]{2,1,0:T(2,128)(2,1)}), bf16[8,2,8192]{2,1,0:T(2,128)(2,1)}, u32[]{:S(2)}, u32[]{:S(2)}) async-start(bf16[8,2,8192]{2,1,0:T(2,128)(2,1)} %reshape.115), calls=%async_computation.1 | async-start | bytes 524288 | tf_op jit(solution)/shard_map/all_to_all | solution.py:89
  56.6 35.3 %all-to-all-start = ((bf16[8,2,32768]{2,1,0:T(2,128)(2,1)}), bf16[8,2,32768]{2,1,0:T(2,128)(2,1)S(1)}, u32[]{:S(2)}, u32[]{:S(2)}) async-start(bf16[8,2,32768]{2,1,0:T(2,128)(2,1)} %reshape.113), calls=%async_computation | async-start | bytes 2097152 | tf_op jit(solution)/shard_map/all_to_all | solution.py:88
  91.9 8.2 %copy-start.6 = (bf16[8,2,32768]{2,1,0:T(2,128)(2,1)}, bf16[8,2,32768]{2,1,0:T(2,128)(2,1)S(1)}, u32[]{:S(2)}) copy-start(bf16[8,2,32768]{2,1,0:T(2,128)(2,1)S(1)} %all-to-all-done) | copy-start | bytes 3145732
  91.9 20.9 %all-to-all-start.2 = ((bf16[8,2,32768]{2,1,0:T(2,128)(2,1)}), bf16[8,2,32768]{2,1,0:T(2,128)(2,1)}, u32[]{:S(2)}, u32[]{:S(2)}) async-start(bf16[8,2,32768]{2,1,0:T(2,128)(2,1)} %reshape.117), calls=%async_computation.2 | async-start | bytes 2097152 | tf_op jit(solution)/shard_map/all_to_all | solution.py:91
  96.7 96.8 %all-gather.2.cloned.1.call-start = ((), (), s32[]{:S(2)}) async-start(), calls=%async_computation.6 | async-start | bytes 9437184 | tf_op jit(solution)/shard_map/all_gather | solution.py:95
  97.4 341.3 %reduce-scatter.4.cloned.1.call-start = ((), (), s32[]{:S(2)}) async-start(), calls=%async_computation.7 | async-start | bytes 6488064
  123.9 10.7 %copy-start.4 = (bf16[2,512,1,4,128]{4,3,1,0,2:T(4,128)(2,1)}, bf16[2,512,1,4,128]{4,3,1,0,2:T(4,128)(2,1)S(1)}, u32[]{:S(2)}) copy-start(bf16[2,512,1,4,128]{4,3,1,0,2:T(4,128)(2,1)S(1)} %get-tuple-element.268) | copy-start | bytes 3145732 | tf_op jit(solution)/shard_map/while
  128.9 3.2 copy-start
  134.9 6.2 copy-start.1
  134.9 6.2 copy-start.10
  144.7 2.0 copy-start.2
  149.2 7.3 %copy-start.3 = (bf16[4,512,1024]{2,1,0:T(8,128)(2,1)S(1)}, bf16[4,512,1024]{2,1,0:T(8,128)(2,1)}, u32[]{:S(2)}) copy-start(bf16[4,512,1024]{2,1,0:T(8,128)(2,1)} %copy-done.2) | copy-start | bytes 12582916 | tf_op jit(solution)/shard_map/while
  149.2 8.1 %copy-start.5 = (bf16[2,512,1,4,128]{4,3,1,0,2:T(4,128)(2,1)S(1)}, bf16[2,512,1,4,128]{4,3,1,0,2:T(4,128)(2,1)}, u32[]{:S(2)}) copy-start(bf16[2,512,1,4,128]{4,3,1,0,2:T(4,128)(2,1)} %copy-done.4) | copy-start | bytes 3145732 | tf_op jit(solution)/shard_map/while
  157.3 10.7 %copy-start.4 = (bf16[2,512,1,4,128]{4,3,1,0,2:T(4,128)(2,1)}, bf16[2,512,1,4,128]{4,3,1,0,2:T(4,128)(2,1)S(1)}, u32[]{:S(2)}) copy-start(bf16[2,512,1,4,128]{4,3,1,0,2:T(4,128)(2,1)S(1)} %get-tuple-element.268) | copy-start | bytes 3145732 | tf_op jit(solution)/shard_map/while
  162.3 3.2 copy-start
  168.3 5.9 copy-start.1
  168.3 5.9 copy-start.10
  182.3 7.3 %copy-start.3 = (bf16[4,512,1024]{2,1,0:T(8,128)(2,1)S(1)}, bf16[4,512,1024]{2,1,0:T(8,128)(2,1)}, u32[]{:S(2)}) copy-start(bf16[4,512,1024]{2,1,0:T(8,128)(2,1)} %copy-done.2) | copy-start | bytes 12582916 | tf_op jit(solution)/shard_map/while
  182.3 8.1 %copy-start.5 = (bf16[2,512,1,4,128]{4,3,1,0,2:T(4,128)(2,1)S(1)}, bf16[2,512,1,4,128]{4,3,1,0,2:T(4,128)(2,1)}, u32[]{:S(2)}) copy-start(bf16[2,512,1,4,128]{4,3,1,0,2:T(4,128)(2,1)} %copy-done.4) | copy-start | bytes 3145732 | tf_op jit(solution)/shard_map/while
  205.8 8.8 %copy-start.7 = (f32[128,768]{1,0:T(8,128)S(1)}, f32[128,768]{1,0:T(8,128)}, u32[]{:S(2)}) copy-start(f32[128,768]{1,0:T(8,128)} %param.15) | copy-start | bytes 1179652
  205.8 9.0 %copy-start.8 = (f32[128,768]{1,0:T(8,128)S(1)}, f32[128,768]{1,0:T(8,128)}, u32[]{:S(2)}) copy-start(f32[128,768]{1,0:T(8,128)} %param.16) | copy-start | bytes 1179652
  205.8 9.1 %copy-start.9 = (f32[128,768]{1,0:T(8,128)S(1)}, f32[128,768]{1,0:T(8,128)}, u32[]{:S(2)}) copy-start(f32[128,768]{1,0:T(8,128)} %param.17) | copy-start | bytes 1179652
  520.0 147.4 %all-to-all-start.4 = ((bf16[32,128,768]{2,1,0:T(8,128)(2,1)}), bf16[32,128,768]{2,1,0:T(8,128)(2,1)}, u32[]{:S(2)}, u32[]{:S(2)}) async-start(bf16[32,128,768]{2,1,0:T(8,128)(2,1)} %stack.2), calls=%async_computation.4 | async-start | bytes 12582912 | tf_op jit(solution)/shard_map/all_to_all | solution.py:117
  (1 other events, 2.0 us)
Sparse Core Ops, SparseCore 0:
  99.4 55.1 all-gather.1
  214.7 223.9 reduce-scatter.3
